TPU v7x, 256 devices: a whole 4x4x8 slice. The times are simulated.
256 devices in a mesh: ctx: 8 (over x, y_hi), chan: 32 (over z, y_lo, core).
Axes of the slice: x: 4, y: 4 (y_hi: 2, y_lo: 2; y = y_hi * 2 + y_lo), z: 8, core: 2. Of those that a mesh axis runs over, the one named last changes fastest.
Arguments:
- inputs: bfloat16 [4096, 4096], P('ctx', 'chan'), may hold values from -6 to 6
- w_in: bfloat16 [4096, 3, 4096], P(None, None, 'chan'), may hold values from -0.09375 to 0.09375
- conv_taps: bfloat16 [3, 3, 4096], P(None, None, 'chan'), may hold values from -3.59375 to 3.59375
- skip_gain: float32 [4096], P('chan'), may hold values from 0.5 to 1.5
- filter_taps: bfloat16 [4096, 4096], P('ctx', 'chan'), may hold values from -0.09375 to 0.09375
- w_out: bfloat16 [4096, 4096], P('chan'), may hold values from -0.1875 to 0.1875
Outputs:
- result: bfloat16 [4096, 4096], P('ctx', 'chan')
All inputs are finite; a program needn't handle non-finite values.
Results may differ from a plain program's by a relative error of at most 0.024.
Values may be sent and summed in bfloat16 or wider, within the bound.
A program may use at most 64 MiB of HBM per device.

v0:
```python
import math
import jax
import jax.numpy as jnp
from jax import lax
from jax.sharding import PartitionSpec as P

KERNEL = 3


def dft_table(double_len):
    step = 32
    hi_ids = jnp.arange(double_len // step, dtype=jnp.int32)[:, None]
    lo_ids = jnp.arange(step, dtype=jnp.int32)[:, None]
    cols = jnp.arange(double_len, dtype=jnp.int32)[None, :]
    scale = 2.0 * math.pi / double_len
    hi_angle = scale * (hi_ids * step * cols % double_len).astype(jnp.float32)
    lo_angle = scale * (lo_ids * cols % double_len).astype(jnp.float32)
    hc, hs = (jnp.cos(hi_angle)[:, None], jnp.sin(hi_angle)[:, None])
    lc, ls = (jnp.cos(lo_angle)[None], jnp.sin(lo_angle)[None])
    cos = (hc * lc - hs * ls).reshape(double_len, double_len)
    sin = (hs * lc + hc * ls).reshape(double_len, double_len)
    return jnp.concatenate([cos, -sin], 0).astype(jnp.bfloat16)


def body(inputs, w_in, conv_taps, skip_gain, filter_taps, w_out):
    span_len, width_dev = inputs.shape
    double_len = 2 * span_len
    groups = lax.axis_size("ctx")
    position = lax.axis_index("ctx")
    own = width_dev // groups
    with jax.named_scope("out_weight_columns"):
        w_cols = lax.all_to_all(w_out, "chan", 1, 0, tiled=True)
    with jax.named_scope("filter_to_owner"):
        taps_t = filter_taps.T.reshape(groups, own, span_len)
        taps_t = lax.all_to_all(taps_t, "ctx", 0, 0, tiled=True)
    with jax.named_scope("input_projection"):
        inputs_t = lax.all_gather(inputs.T, "chan", axis=0, tiled=True)
        w_flat = w_in.reshape(w_in.shape[0], 3 * width_dev)
        proj_t = lax.dot_general(
            w_flat, inputs_t, (((0,), (0,)), ((), ())), preferred_element_type=jnp.float32
        ).astype(jnp.bfloat16)
    with jax.named_scope("projection_to_owner"):
        proj_t = proj_t.reshape(3, groups, own, span_len)
        proj_t = lax.all_to_all(proj_t, "ctx", 1, 1, tiled=True)
    with jax.named_scope("short_conv"):
        start = position * own
        taps = lax.dynamic_slice_in_dim(conv_taps, start, own, axis=2)
        rim = jnp.pad(
            proj_t[:, :-1, :, span_len - (KERNEL - 1) :], ((0, 0), (1, 0), (0, 0), (0, 0))
        )
        padded = jnp.concatenate([rim, proj_t], 3)
        filtered = jnp.zeros(proj_t.shape, jnp.float32)
        for lag in range(KERNEL):
            start_row = KERNEL - 1 - lag
            filtered = filtered + taps[lag].astype(jnp.float32)[:, None, :, None] * padded[
                ..., start_row : start_row + span_len
            ].astype(jnp.float32)
        streams = filtered.astype(jnp.bfloat16)
        gate_out = streams[0]
        gated_in = (streams[1].astype(jnp.float32) * streams[2].astype(jnp.float32)).astype(
            jnp.bfloat16
        )
    with jax.named_scope("spectra"):
        table = dft_table(double_len)
        forward_in = table[:, :span_len]
        spectra_in = jnp.einsum(
            "jdb,fb->jdf", gated_in, forward_in, preferred_element_type=jnp.float32
        ).astype(jnp.bfloat16)
        previous = jnp.pad(taps_t[:-1, :, 1:], ((1, 0), (0, 0), (0, 0)))
        padded_taps = jnp.concatenate(
            [taps_t, jnp.zeros((groups, own, 1), jnp.bfloat16), previous], 2
        )
        spectra_taps = jnp.einsum(
            "kdm,fm->kdf", padded_taps, table, preferred_element_type=jnp.float32
        ).astype(jnp.bfloat16)
    with jax.named_scope("mixture"):
        real_g = spectra_taps[:, :, :double_len].astype(jnp.float32)
        imag_g = spectra_taps[:, :, double_len:].astype(jnp.float32)
        real_u = spectra_in[:, :, :double_len].astype(jnp.float32)
        imag_u = spectra_in[:, :, double_len:].astype(jnp.float32)
        mixed = []
        for target in range(groups):
            acc_r = jnp.zeros((own, double_len), jnp.float32)
            acc_i = jnp.zeros((own, double_len), jnp.float32)
            for source in range(target + 1):
                lag = target - source
                acc_r = acc_r + (real_g[lag] * real_u[source] - imag_g[lag] * imag_u[source])
                acc_i = acc_i + (real_g[lag] * imag_u[source] + imag_g[lag] * real_u[source])
            mixed.append(jnp.concatenate([acc_r, acc_i], 1))
        mixture = jnp.stack(mixed, 0).astype(jnp.bfloat16)
    with jax.named_scope("inverse_and_gate"):
        long_out = jnp.einsum(
            "idf,fa->ida", mixture, forward_in, preferred_element_type=jnp.float32
        ) * (1.0 / double_len)
        gain = lax.dynamic_slice_in_dim(skip_gain, start, own)
        long_out = long_out + gain[None, :, None] * gated_in.astype(jnp.float32)
        gated_out = (gate_out.astype(jnp.float32) * long_out).astype(jnp.bfloat16)
    with jax.named_scope("gated_back_to_rows"):
        gated_out = lax.all_to_all(gated_out, "ctx", 0, 0, tiled=True)
        gated_out = gated_out.reshape(width_dev, span_len)
    with jax.named_scope("output_projection"):
        gathered = lax.all_gather(gated_out, "chan", axis=0, tiled=True)
        result = lax.dot_general(
            gathered, w_cols, (((0,), (0,)), ((), ())), preferred_element_type=jnp.float32
        ).astype(jnp.bfloat16)
    return result


def solution(mesh):
    return jax.shard_map(
        body,
        mesh=mesh,
        in_specs=(
            P("ctx", "chan"),
            P(None, None, "chan"),
            P(None, None, "chan"),
            P("chan"),
            P("ctx", "chan"),
            P("chan", None),
        ),
        out_specs=P("ctx", "chan"),
        check_vma=False,
    )
```

profile of v0, /device:TPU:1, one launch (start us, length us, event | category | flops | bytes accessed | tf_op | source)
XLA Modules:
  0.0 208.1 jit_solution(4928286048202900547)
XLA Ops:
  6.5 0.0 copy-start
  6.5 0.0 all-gather.3.cloned.1.call-start
  6.5 0.7 all-gather.3.cloned.1.call-update
  7.3 1.9 copy.19
  9.1 7.5 %all-to-all-start.1 = ((bf16[8,16,512]{2,1,0:T(8,128)(2,1)}), bf16[8,16,512]{2,1,0:T(8,128)(2,1)S(1)}, u32[]{:S(2)}, u32[]{:S(2)}) async-start(bf16[8,16,512]{2,1,0:T(8,128)(2,1)} %bitcast.8), calls=%async_computation.1 | async-start | bytes 262144 | tf_op jit(solution)/shard_map/filter_to_owner/all_to_all | solution.py:35
  16.6 0.5 fusion.45
  17.2 0.6 fusion.48
  17.8 3.5 %negate_convert_fusion = (bf16[32,32,1024]{2,1,0:T(8,128)(2,1)}, bf16[32,32,1024]{2,1,0:T(8,128)(2,1)}) fusion(f32[32,1024]{1,0:T(8,128)S(1)} %get-tuple-element.22, f32[32,1024]{1,0:T(8,128)S(1)} %get-tuple-element.21, f32[32,1024]{1,0:T(8,128)S(1)} %get-tuple-element.23, f32[32,1024]{1,0:T(8,128)S(1)} %get-tuple-element.20), kind=kLoop, calls=%fused_computation.5 | loop fusion | flops 9437184 | bytes 4718592 | tf_op jit(solution)/shard_map/convert.44
  21.3 0.0 copy-start.6
  21.3 0.0 copy-start.5
  21.3 0.0 copy-done
  21.3 2.9 %copy.14 = bf16[4096,3,128]{0,2,1:T(8,128)(2,1)} copy(bf16[4096,3,128]{2,0,1:T(8,128)(2,1)S(1)} %copy-done) | data formatting | bytes 6291456 | tf_op args[1]
  24.2 0.0 copy-done.6
  24.2 0.1 dynamic_slice.7
  24.3 0.0 copy-done.5
  24.3 0.1 fusion.68
  24.3 0.0 all-to-all-done.1
  24.4 0.0 copy-start.4
  24.4 0.1 slice.145
  24.5 61.2 %all-gather.3.cloned.1.call-done = bf16[4096,512]{0,1:T(8,128)(2,1)} async-done(((bf16[128,512]{0,1:T(8,128)(2,1)}), bf16[4096,512]{0,1:T(8,128)(2,1)}) %all-gather.3.cloned.1.call-update) | async-done | bytes 4194320 | tf_op jit(solution)/shard_map/input_projection/all_gather | solution.py:37
  85.6 0.0 copy-start.1
  85.6 5.1 %convolution_convert_fusion.1 = bf16[384,512]{1,0:T(8,128)(2,1)S(1)} fusion(bf16[4096,384]{0,1:T(8,128)(2,1)} %bitcast.117, bf16[4096,512]{0,1:T(8,128)(2,1)} %all-gather.3.cloned.1.call-done), kind=kOutput, calls=%fused_computation.11 | convolution fusion | flops 1610809344 | bytes 7733248 | tf_op jit(solution)/shard_map/input_projection/dot_general | solution.py:39
  90.7 0.0 copy-done.4
  90.7 0.8 copy.15
  91.5 6.4 %all-to-all-start = ((bf16[3,8,16,512]{3,2,0,1:T(8,128)(2,1)}), bf16[3,8,16,512]{3,2,0,1:T(8,128)(2,1)S(1)}, u32[]{:S(2)}, u32[]{:S(2)}) async-start(bf16[3,8,16,512]{3,2,0,1:T(8,128)(2,1)} %copy.15), calls=%async_computation | async-start | bytes 786432 | tf_op jit(solution)/shard_map/projection_to_owner/all_to_all | solution.py:44
  97.9 0.0 all-gather.5.cloned.1.call-start
  97.9 0.0 copy-done.1
  97.9 3.2 %fusion.3 = bf16[8,16,2048]{2,1,0:T(8,128)(2,1)S(1)} fusion(bf16[1024,1024]{1,0:T(8,128)(2,1)S(1)} %bitcast.118, bf16[1024,1024]{1,0:T(8,128)(2,1)} %bitcast.121, bf16[7,16,511]{2,1,0:T(8,128)(2,1)S(1)} %slice.145, bf16[8,16,512]{2,1,0:T(8,128)(2,1)} %copy-done.4, bf16[1024]{0:T(1024)(128)(2,1)S(1)} %pad.29.clone), kind=kOutput, calls=%fused_computation.7 | convolution fusion | flops 546570240 | bytes 4966176 | tf_op jit(solution)/shard_map/spectra/kdm,fm->kdf/dot_general | solution.py:73
  101.1 0.1 slice_convert_fusion.3
  101.2 6.1 %all-to-all-done = bf16[3,8,16,512]{3,2,0,1:T(8,128)(2,1)S(1)} async-done(((bf16[3,8,16,512]{3,2,0,1:T(8,128)(2,1)}), bf16[3,8,16,512]{3,2,0,1:T(8,128)(2,1)S(1)}, u32[]{:S(2)}, u32[]{:S(2)}) %all-to-all-start) | async-done | bytes 393248 | tf_op jit(solution)/shard_map/projection_to_owner/all_to_all | solution.py:44
  107.3 0.1 slice.141
  107.4 0.2 fusion.13
  107.7 0.4 add_convert_fusion
  108.0 2.0 convolution_convert_fusion
  110.1 0.1 slice_convert_fusion.2
  110.2 0.2 fusion.63
  110.4 0.2 fusion.64
  110.5 0.1 fusion.61
  110.7 0.1 fusion.62
  110.8 0.1 fusion.59
  110.9 0.1 fusion.60
  111.1 0.0 copy-start.2
  111.1 0.1 fusion.57
  111.1 0.1 fusion.58
  111.2 0.1 fusion.55
  111.3 0.1 fusion.56
  111.4 0.1 fusion.54
  111.5 0.1 fusion.53
  111.5 0.0 copy-start.3
  111.7 1.0 copy-done.2
  112.6 0.5 fusion.10
  113.1 9.8 %all_to_all.34 = bf16[8,16,512]{2,1,0:T(8,128)(2,1)} all-to-all(bf16[8,16,512]{2,1,0:T(8,128)(2,1)S(1)} %fusion.10), channel_id=1, replica_groups=mesh['ctx'=8,'chan'=32] {'ctx'}, dimensions={0} | all-to-all | bytes 262144 | tf_op jit(solution)/shard_map/gated_back_to_rows/all_to_all | solution.py:99
  122.9 0.0 all-gather.5.cloned.1.call-update
  123.0 0.0 copy-done.3
  123.0 0.7 copy.20
  123.7 44.2 %all_to_all.35 = bf16[128,32,128]{0,2,1:T(8,128)(2,1)S(1)} all-to-all(bf16[128,32,128]{0,2,1:T(8,128)(2,1)S(1)} %bitcast.116), channel_id=1, replica_groups=mesh['ctx'=8,'chan'=32] {'chan'}, dimensions={1} | all-to-all | bytes 2097152 | tf_op jit(solution)/shard_map/out_weight_columns/all_to_all | solution.py:32
  167.9 0.7 copy.21
  168.6 28.6 %all-gather.5.cloned.1.call-done = bf16[4096,512]{1,0:T(8,128)(2,1)} async-done(((bf16[128,512]{1,0:T(8,128)(2,1)}), bf16[4096,512]{1,0:T(8,128)(2,1)}) %all-gather.5.cloned.1.call-update) | async-done | bytes 4194320 | tf_op jit(solution)/shard_map/output_projection/all_gather | solution.py:102
  197.1 4.1 %convolution_convert_fusion.2 = bf16[512,128]{1,0:T(8,128)(2,1)} fusion(bf16[4096,512]{1,0:T(8,128)(2,1)} %all-gather.5.cloned.1.call-done, bf16[4096,128]{1,0:T(8,128)(2,1)S(1)} %bitcast.124), kind=kOutput, calls=%fused_computation.15 | convolution fusion | flops 536936448 | bytes 5373952 | tf_op jit(solution)/shard_map/output_projection/dot_general | solution.py:103
  (12 shorter events, 0.1 us)
Async XLA Ops:
  6.5 14.8 %copy-start = (bf16[4096,3,128]{2,0,1:T(8,128)(2,1)S(1)}, bf16[4096,3,128]{2,0,1:T(8,128)(2,1)}, u32[]{:S(2)}) copy-start(bf16[4096,3,128]{2,0,1:T(8,128)(2,1)} %param.7) | copy-start | bytes 9437188
  6.5 79.1 %all-gather.3.cloned.1.call-start = ((), (), s32[]{:S(2)}) async-start(), calls=%async_computation.4 | async-start | bytes 4325376 | tf_op jit(solution)/shard_map/input_projection/all_gather | solution.py:37
  9.1 15.2 %all-to-all-start.1 = ((bf16[8,16,512]{2,1,0:T(8,128)(2,1)}), bf16[8,16,512]{2,1,0:T(8,128)(2,1)S(1)}, u32[]{:S(2)}, u32[]{:S(2)}) async-start(bf16[8,16,512]{2,1,0:T(8,128)(2,1)} %bitcast.8), calls=%async_computation.1 | async-start | bytes 262144 | tf_op jit(solution)/shard_map/filter_to_owner/all_to_all | solution.py:35
  21.3 2.9 %copy-start.6 = (f32[128]{0:T(128)S(1)}, f32[128]{0:T(128)}, u32[]{:S(2)}) copy-start(f32[128]{0:T(128)} %param.9) | copy-start | bytes 1540
  21.3 3.0 %copy-start.5 = (bf16[3,3,128]{2,1,0:T(4,128)(2,1)S(1)}, bf16[3,3,128]{2,1,0:T(4,128)(2,1)}, u32[]{:S(2)}) copy-start(bf16[3,3,128]{2,1,0:T(4,128)(2,1)} %param.8) | copy-start | bytes 6916
  24.4 66.4 %copy-start.4 = (bf16[8,16,512]{2,1,0:T(8,128)(2,1)}, bf16[8,16,512]{2,1,0:T(8,128)(2,1)S(1)}, u32[]{:S(2)}) copy-start(bf16[8,16,512]{2,1,0:T(8,128)(2,1)S(1)} %all-to-all-done.1) | copy-start | bytes 393220
  85.6 12.3 %copy-start.1 = (bf16[32,32,1024]{2,1,0:T(8,128)(2,1)S(1)}, bf16[32,32,1024]{2,1,0:T(8,128)(2,1)}, u32[]{:S(2)}) copy-start(bf16[32,32,1024]{2,1,0:T(8,128)(2,1)} %get-tuple-element.15) | copy-start | bytes 6291460
  91.5 15.8 %all-to-all-start = ((bf16[3,8,16,512]{3,2,0,1:T(8,128)(2,1)}), bf16[3,8,16,512]{3,2,0,1:T(8,128)(2,1)S(1)}, u32[]{:S(2)}, u32[]{:S(2)}) async-start(bf16[3,8,16,512]{3,2,0,1:T(8,128)(2,1)} %copy.15), calls=%async_computation | async-start | bytes 786432 | tf_op jit(solution)/shard_map/projection_to_owner/all_to_all | solution.py:44
  97.9 99.3 %all-gather.5.cloned.1.call-start = ((), (), s32[]{:S(2)}) async-start(), calls=%async_computation.5 | async-start | bytes 4325376 | tf_op jit(solution)/shard_map/output_projection/all_gather | solution.py:102
  111.1 1.6 copy-start.2
  111.5 11.4 %copy-start.3 = (bf16[128,4096]{1,0:T(8,128)(2,1)S(1)}, bf16[128,4096]{1,0:T(8,128)(2,1)}, u32[]{:S(2)}) copy-start(bf16[128,4096]{1,0:T(8,128)(2,1)} %param.11) | copy-start | bytes 3145732
Sparse Core Ops, SparseCore 0:
  9.1 76.4 all-gather.2
  123.1 74.0 all-gather.4
where the time goes:
time: 209 us; the launch traced here: 208 us
  waiting for transfers between devices  96.6 us (46%)
  blocking collectives  54.1 us (26%)
  matrix products  14.9 us (7%)
  starting transfers between devices  13.9 us (7%)
  between operations  13.7 us (7%)
  local copies, waits for them, and re-layouts  8.15 us (4%)
  other arithmetic  6.84 us (3%)
    all_gather x1, waiting for transfers between devices, body(): inputs_t = lax.all_gather(inputs.T, 'chan', axis=0, tiled=True)  61.2 us
    all_to_all x1, blocking collectives, body(): w_cols = lax.all_to_all(w_out, 'chan', 1, 0, tiled=True)  44.2 us
    all_gather x1, waiting for transfers between devices, body(): gathered = lax.all_gather(gated_out, 'chan', axis=0, tiled=True)  28.6 us
    all_to_all x1, blocking collectives, body(): gated_out = lax.all_to_all(gated_out, 'ctx', 0, 0, tiled=True)  9.83 us
    all_to_all x1, starting transfers between devices, body(): taps_t = lax.all_to_all(taps_t, 'ctx', 0, 0, tiled=True)  7.48 us
    all_to_all x1, starting transfers between devices, body(): proj_t = lax.all_to_all(proj_t, 'ctx', 1, 1, tiled=True)  6.35 us
    all_to_all x1, waiting for transfers between devices, body(): proj_t = lax.all_to_all(proj_t, 'ctx', 1, 1, tiled=True)  6.07 us
    dot_general x1, matrix products, body(): lax.dot_general(w_flat, inputs_t, (((0,), (0,)), ((), ())), preferred_ele...  5.1 us
  transfers between devices with their start and end apart: 4, of which 3 were waited for; matrix products, arithmetic and copies ran while one was open for 7% of the time, Pallas kernels for 0%

commit v1 on v0

--- a/solution.py
+++ b/solution.py
@@ -29,7 +29,10 @@
     position = lax.axis_index("ctx")
     own = width_dev // groups
     with jax.named_scope("out_weight_columns"):
-        w_cols = lax.all_to_all(w_out, "chan", 1, 0, tiled=True)
+        size = lax.axis_size("chan")
+        blocks = jnp.stack(jnp.split(w_out, size, axis=1), axis=0)
+        blocks = lax.all_to_all(blocks, "chan", split_axis=0, concat_axis=0)
+        w_cols = jnp.concatenate(blocks, axis=0)
     with jax.named_scope("filter_to_owner"):
         taps_t = filter_taps.T.reshape(groups, own, span_len)
         taps_t = lax.all_to_all(taps_t, "ctx", 0, 0, tiled=True)

time: 209 us -> 211 us (level)
  local copies, waits for them, and re-layouts: 8.15 us -> 29.7 us
  waiting for transfers between devices: 96.6 us -> 83.6 us
  blocking collectives: 54.1 us -> 43.3 us
  starting transfers between devices: 13.9 us -> 17.2 us
    unnamed x17 -> x49, local copies, waits for them, and re-layouts: 4.57 us -> 26.1 us
    all_gather x1, waiting for transfers between devices: 28.6 us -> 13.7 us  [body(): gathered = lax.all_gather(gated_out, 'chan', axis=0, tiled=True)]
    all_to_all x2 -> x1, blocking collectives: 54.1 us -> 43.3 us  [body(): blocks = lax.all_to_all(blocks, 'chan', split_axis=0, concat_axis=0)]
    all_to_all x0 -> x1, waiting for transfers between devices: none -> 6.03 us  [body(): gated_out = lax.all_to_all(gated_out, 'ctx', 0, 0, tiled=True)]
    all_gather x1, waiting for transfers between devices: 61.2 us -> 57 us  [body(): inputs_t = lax.all_gather(inputs.T, 'chan', axis=0, tiled=True)]
    all_to_all x0 -> x1, starting transfers between devices: none -> 3.37 us  [body(): gated_out = lax.all_to_all(gated_out, 'ctx', 0, 0, tiled=True)]
  transfers between devices with their start and end apart: 4 -> 5, of which waited for: 3 -> 4; matrix products, arithmetic and copies ran while one was open for 7% -> 17% of each run, Pallas kernels for 0% -> 0%
where the time goes in v1:
time: 211 us; the launch traced here: 210 us
  waiting for transfers between devices  83.6 us (40%)
  blocking collectives  43.3 us (21%)
  local copies, waits for them, and re-layouts  29.7 us (14%)
  starting transfers between devices  17.2 us (8%)
  matrix products  15.6 us (7%)
  between operations  13.7 us (6%)
  other arithmetic  6.83 us (3%)
    all_gather x1, waiting for transfers between devices, body(): inputs_t = lax.all_gather(inputs.T, 'chan', axis=0, tiled=True)  57 us
    all_to_all x1, blocking collectives, body(): blocks = lax.all_to_all(blocks, 'chan', split_axis=0, concat_axis=0)  43.3 us
    unnamed x49, local copies, waits for them, and re-layouts  26.1 us
    all_gather x1, waiting for transfers between devices, body(): gathered = lax.all_gather(gated_out, 'chan', axis=0, tiled=True)  13.7 us
    all_to_all x1, starting transfers between devices, body(): taps_t = lax.all_to_all(taps_t, 'ctx', 0, 0, tiled=True)  7.48 us
    all_to_all x1, starting transfers between devices, body(): proj_t = lax.all_to_all(proj_t, 'ctx', 1, 1, tiled=True)  6.35 us
    all_to_all x1, waiting for transfers between devices, body(): proj_t = lax.all_to_all(proj_t, 'ctx', 1, 1, tiled=True)  6.12 us
    all_to_all x1, waiting for transfers between devices, body(): gated_out = lax.all_to_all(gated_out, 'ctx', 0, 0, tiled=True)  6.03 us
  transfers between devices with their start and end apart: 5, of which 4 were waited for; matrix products, arithmetic and copies ran while one was open for 17% of the time, Pallas kernels for 0%

profile of v1, /device:TPU:1, one launch (start us, length us, event | category | flops | bytes accessed | tf_op | source)
XLA Modules:
  0.0 210.0 jit_solution(15848799606438609231)
XLA Ops:
  6.5 0.7 all-gather.3.cloned.1.call-update
  7.3 1.9 copy.15
  9.1 7.5 %all-to-all-start.1 = ((bf16[8,16,512]{2,1,0:T(8,128)(2,1)}), bf16[8,16,512]{2,1,0:T(8,128)(2,1)S(1)}, u32[]{:S(2)}, u32[]{:S(2)}) async-start(bf16[8,16,512]{2,1,0:T(8,128)(2,1)} %bitcast.8), calls=%async_computation.1 | async-start | bytes 262144 | tf_op jit(solution)/shard_map/filter_to_owner/all_to_all | solution.py:38
  16.6 0.5 fusion.37
  17.2 1.4 constant_dynamic-update-slice_fusion.39
  18.5 1.4 constant_dynamic-update-slice_fusion.38
  19.9 0.6 fusion.40
  20.5 3.5 %negate_convert_fusion = (bf16[32,32,1024]{2,1,0:T(8,128)(2,1)}, bf16[32,32,1024]{2,1,0:T(8,128)(2,1)}) fusion(f32[32,1024]{1,0:T(8,128)S(1)} %get-tuple-element.22, f32[32,1024]{1,0:T(8,128)S(1)} %get-tuple-element.21, f32[32,1024]{1,0:T(8,128)S(1)} %get-tuple-element.23, f32[32,1024]{1,0:T(8,128)S(1)} %get-tuple-element.20), kind=kLoop, calls=%fused_computation.5 | loop fusion | flops 9437184 | bytes 4718592 | tf_op jit(solution)/shard_map/convert.44
  24.0 1.4 constant_dynamic-update-slice_fusion.37
  25.4 2.9 %copy.10 = bf16[4096,3,128]{0,2,1:T(8,128)(2,1)} copy(bf16[4096,3,128]{2,0,1:T(8,128)(2,1)S(1)} %copy-done) | data formatting | bytes 6291456 | tf_op args[1]
  28.6 57.0 %all-gather.3.cloned.1.call-done = bf16[4096,512]{0,1:T(8,128)(2,1)} async-done(((bf16[128,512]{0,1:T(8,128)(2,1)}), bf16[4096,512]{0,1:T(8,128)(2,1)}) %all-gather.3.cloned.1.call-update) | async-done | bytes 4194320 | tf_op jit(solution)/shard_map/input_projection/all_gather | solution.py:40
  85.6 5.1 %convolution_convert_fusion.1 = bf16[384,512]{1,0:T(8,128)(2,1)S(1)} fusion(bf16[4096,384]{0,1:T(8,128)(2,1)} %bitcast.177, bf16[4096,512]{0,1:T(8,128)(2,1)} %all-gather.3.cloned.1.call-done), kind=kOutput, calls=%fused_computation.11 | convolution fusion | flops 1610809344 | bytes 7733248 | tf_op jit(solution)/shard_map/input_projection/dot_general | solution.py:42
  90.7 0.8 copy.11
  91.5 6.4 %all-to-all-start = ((bf16[3,8,16,512]{3,2,0,1:T(8,128)(2,1)}), bf16[3,8,16,512]{3,2,0,1:T(8,128)(2,1)S(1)}, u32[]{:S(2)}, u32[]{:S(2)}) async-start(bf16[3,8,16,512]{3,2,0,1:T(8,128)(2,1)} %copy.11), calls=%async_computation | async-start | bytes 786432 | tf_op jit(solution)/shard_map/projection_to_owner/all_to_all | solution.py:47
  97.9 3.2 %fusion.3 = bf16[8,16,2048]{2,1,0:T(8,128)(2,1)S(1)} fusion(bf16[1024,1024]{1,0:T(8,128)(2,1)S(1)} %bitcast.178, bf16[1024,1024]{1,0:T(8,128)(2,1)} %bitcast.181, bf16[7,16,511]{2,1,0:T(8,128)(2,1)S(1)} %slice.145, bf16[8,16,512]{2,1,0:T(8,128)(2,1)} %copy-done.5, bf16[1024]{0:T(1024)(128)(2,1)S(1)} %pad.29.clone), kind=kOutput, calls=%fused_computation.7 | convolution fusion | flops 546570240 | bytes 4966176 | tf_op jit(solution)/shard_map/spectra/kdm,fm->kdf/dot_general | solution.py:76
  101.1 0.1 slice_convert_fusion.3
  101.2 6.1 %all-to-all-done = bf16[3,8,16,512]{3,2,0,1:T(8,128)(2,1)S(1)} async-done(((bf16[3,8,16,512]{3,2,0,1:T(8,128)(2,1)}), bf16[3,8,16,512]{3,2,0,1:T(8,128)(2,1)S(1)}, u32[]{:S(2)}, u32[]{:S(2)}) %all-to-all-start) | async-done | bytes 393248 | tf_op jit(solution)/shard_map/projection_to_owner/all_to_all | solution.py:47
  107.4 0.2 fusion.13
  107.7 0.4 add_convert_fusion
  108.0 2.0 convolution_convert_fusion
  110.1 0.1 slice_convert_fusion.2
  110.2 0.2 fusion.55
  110.4 0.2 fusion.56
  110.6 0.1 fusion.53
  110.7 0.1 fusion.54
  110.8 0.1 fusion.51
  111.0 0.1 fusion.52
  111.7 1.0 copy-done.2
  112.7 1.1 fusion.10
  113.8 3.4 %all-to-all-start.2 = ((bf16[8,16,512]{2,1,0:T(8,128)(2,1)}), bf16[8,16,512]{2,1,0:T(8,128)(2,1)S(1)}, u32[]{:S(2)}, u32[]{:S(2)}) async-start(bf16[8,16,512]{2,1,0:T(8,128)(2,1)} %fusion.10), calls=%async_computation.2 | async-start | bytes 262144 | tf_op jit(solution)/shard_map/gated_back_to_rows/all_to_all | solution.py:102
  117.2 0.6 constant_dynamic-update-slice_fusion.36
  117.8 6.0 %all-to-all-done.2 = bf16[8,16,512]{2,1,0:T(8,128)(2,1)S(1)} async-done(((bf16[8,16,512]{2,1,0:T(8,128)(2,1)}), bf16[8,16,512]{2,1,0:T(8,128)(2,1)S(1)}, u32[]{:S(2)}, u32[]{:S(2)}) %all-to-all-start.2) | async-done | bytes 131104 | tf_op jit(solution)/shard_map/gated_back_to_rows/all_to_all | solution.py:102
  123.9 0.7 copy-done.4
  124.5 0.6 constant_dynamic-update-slice_fusion.35
  125.2 0.6 constant_dynamic-update-slice_fusion.34
  125.8 0.6 constant_dynamic-update-slice_fusion.33
  126.4 0.6 constant_dynamic-update-slice_fusion.32
  127.0 0.6 constant_dynamic-update-slice_fusion.31
  127.6 0.6 constant_dynamic-update-slice_fusion.30
  128.3 0.6 constant_dynamic-update-slice_fusion.29
  128.9 0.6 constant_dynamic-update-slice_fusion.28
  129.5 0.6 constant_dynamic-update-slice_fusion.27
  130.1 0.6 constant_dynamic-update-slice_fusion.26
  130.7 0.6 constant_dynamic-update-slice_fusion.25
  131.4 0.6 constant_dynamic-update-slice_fusion.24
  132.0 0.6 constant_dynamic-update-slice_fusion.23
  132.6 0.6 constant_dynamic-update-slice_fusion.22
  133.2 0.6 constant_dynamic-update-slice_fusion.21
  133.9 0.6 constant_dynamic-update-slice_fusion.20
  134.5 0.6 constant_dynamic-update-slice_fusion.19
  135.1 0.6 constant_dynamic-update-slice_fusion.18
  135.8 0.6 constant_dynamic-update-slice_fusion.17
  136.4 0.6 constant_dynamic-update-slice_fusion.16
  137.0 0.6 constant_dynamic-update-slice_fusion.15
  137.6 0.6 constant_dynamic-update-slice_fusion.14
  138.2 0.6 constant_dynamic-update-slice_fusion.13
  138.9 0.6 constant_dynamic-update-slice_fusion.12
  139.5 0.6 constant_dynamic-update-slice_fusion.11
  140.1 0.6 constant_dynamic-update-slice_fusion.10
  140.7 0.6 constant_dynamic-update-slice_fusion.9
  141.4 0.6 constant_dynamic-update-slice_fusion.8
  142.0 43.3 %all_to_all.20 = bf16[32,128,128]{2,1,0:T(8,128)(2,1)S(1)} all-to-all(bf16[32,128,128]{2,1,0:T(8,128)(2,1)} %constant_dynamic-update-slice_fusion.8), channel_id=1, replica_groups=mesh['ctx'=8,'chan'=32] {'chan'}, dimensions={0} | all-to-all | bytes 2097152 | tf_op jit(solution)/shard_map/out_weight_columns/all_to_all | solution.py:34
  185.3 13.7 %all-gather.5.cloned.1.call-done = bf16[4096,512]{1,0:T(8,128)(2,1)} async-done(((bf16[128,512]{1,0:T(8,128)(2,1)}), bf16[4096,512]{1,0:T(8,128)(2,1)}) %all-gather.5.cloned.1.call-update) | async-done | bytes 4194320 | tf_op jit(solution)/shard_map/output_projection/all_gather | solution.py:105
  199.0 4.1 %convolution_convert_fusion.2 = bf16[512,128]{1,0:T(8,128)(2,1)} fusion(bf16[4096,512]{1,0:T(8,128)(2,1)} %all-gather.5.cloned.1.call-done, bf16[4096,128]{1,0:T(8,128)(2,1)S(1)} %bitcast.184), kind=kOutput, calls=%fused_computation.15 | convolution fusion | flops 536936448 | bytes 5373952 | tf_op jit(solution)/shard_map/output_projection/dot_general | solution.py:106
  (40 shorter events, 0.9 us)
Async XLA Ops:
  6.5 18.9 %copy-start = (bf16[4096,3,128]{2,0,1:T(8,128)(2,1)S(1)}, bf16[4096,3,128]{2,0,1:T(8,128)(2,1)}, u32[]{:S(2)}) copy-start(bf16[4096,3,128]{2,0,1:T(8,128)(2,1)} %param.7) | copy-start | bytes 9437188
  6.5 79.1 %all-gather.3.cloned.1.call-start = ((), (), s32[]{:S(2)}) async-start(), calls=%async_computation.4 | async-start | bytes 4325376 | tf_op jit(solution)/shard_map/input_projection/all_gather | solution.py:40
  9.1 19.4 %all-to-all-start.1 = ((bf16[8,16,512]{2,1,0:T(8,128)(2,1)}), bf16[8,16,512]{2,1,0:T(8,128)(2,1)S(1)}, u32[]{:S(2)}, u32[]{:S(2)}) async-start(bf16[8,16,512]{2,1,0:T(8,128)(2,1)} %bitcast.8), calls=%async_computation.1 | async-start | bytes 262144 | tf_op jit(solution)/shard_map/filter_to_owner/all_to_all | solution.py:38
  24.0 4.3 %copy-start.7 = (f32[128]{0:T(128)S(1)}, f32[128]{0:T(128)}, u32[]{:S(2)}) copy-start(f32[128]{0:T(128)} %param.9) | copy-start | bytes 1540
  24.0 4.4 %copy-start.6 = (bf16[3,3,128]{2,1,0:T(4,128)(2,1)S(1)}, bf16[3,3,128]{2,1,0:T(4,128)(2,1)}, u32[]{:S(2)}) copy-start(bf16[3,3,128]{2,1,0:T(4,128)(2,1)} %param.8) | copy-start | bytes 6916
  28.5 62.2 %copy-start.5 = (bf16[8,16,512]{2,1,0:T(8,128)(2,1)}, bf16[8,16,512]{2,1,0:T(8,128)(2,1)S(1)}, u32[]{:S(2)}) copy-start(bf16[8,16,512]{2,1,0:T(8,128)(2,1)S(1)} %all-to-all-done.1) | copy-start | bytes 393220
  85.6 12.3 %copy-start.1 = (bf16[32,32,1024]{2,1,0:T(8,128)(2,1)S(1)}, bf16[32,32,1024]{2,1,0:T(8,128)(2,1)}, u32[]{:S(2)}) copy-start(bf16[32,32,1024]{2,1,0:T(8,128)(2,1)} %get-tuple-element.15) | copy-start | bytes 6291460
  91.5 15.8 %all-to-all-start = ((bf16[3,8,16,512]{3,2,0,1:T(8,128)(2,1)}), bf16[3,8,16,512]{3,2,0,1:T(8,128)(2,1)S(1)}, u32[]{:S(2)}, u32[]{:S(2)}) async-start(bf16[3,8,16,512]{3,2,0,1:T(8,128)(2,1)} %copy.11), calls=%async_computation | async-start | bytes 786432 | tf_op jit(solution)/shard_map/projection_to_owner/all_to_all | solution.py:47
  111.1 1.6 copy-start.2
  111.5 5.7 %copy-start.3 = (bf16[128,4096]{1,0:T(8,128)(2,1)S(1)}, bf16[128,4096]{1,0:T(8,128)(2,1)}, u32[]{:S(2)}) copy-start(bf16[128,4096]{1,0:T(8,128)(2,1)} %param.11) | copy-start | bytes 3145732
  113.8 10.1 %all-to-all-start.2 = ((bf16[8,16,512]{2,1,0:T(8,128)(2,1)}), bf16[8,16,512]{2,1,0:T(8,128)(2,1)S(1)}, u32[]{:S(2)}, u32[]{:S(2)}) async-start(bf16[8,16,512]{2,1,0:T(8,128)(2,1)} %fusion.10), calls=%async_computation.2 | async-start | bytes 262144 | tf_op jit(solution)/shard_map/gated_back_to_rows/all_to_all | solution.py:102
  117.2 81.8 %all-gather.5.cloned.1.call-start = ((), (), s32[]{:S(2)}) async-start(), calls=%async_computation.5 | async-start | bytes 4325376 | tf_op jit(solution)/shard_map/output_projection/all_gather | solution.py:105
  123.9 0.7 copy-start.4
Sparse Core Ops, SparseCore 0:
  9.1 76.4 all-gather.2
  124.7 74.2 all-gather.4
